TPU v7x, 32 devices: a whole 2x2x4 slice. The times are simulated.
32 devices in a mesh: rollout: 2 (over y), branch: 4 (over z), seq: 4 (over x, core).
Axes of the slice: x: 2, y: 2, z: 4, core: 2. Of those that a mesh axis runs over, the one named last changes fastest.
Arguments:
- queries: bfloat16 [8, 512, 4096], P(('rollout', 'branch'), 'seq'), parts along dimension 0, may hold values from -8 to 8
- keyvals: bfloat16 [8, 512, 2, 256], P(('rollout', 'branch'), 'seq'), parts along dimension 0, may hold values from -4 to 4
- residual: bfloat16 [8, 512, 4096], P(('rollout', 'branch'), 'seq'), parts along dimension 0, may hold values from -3 to 3
- read_list: int32 [8, 4, 3], P(('rollout', 'branch'), 'seq'), parts along dimension 0, may hold values from 0 to 3
- router: bfloat16 [4096, 8], replicated, may hold values from -0.09375 to 0.09375
- expert_ids: int32 [8, 512, 2], P(('rollout', 'branch'), 'seq'), parts along dimension 0, may hold values from 0 to 7, all different within a row; in each aligned block of 128 rows (0 to 127, 128 to 255, ..., all dimensions but the last counted through in order) at most 48 rows name the same one
- w_gate_up: bfloat16 [16, 4096, 2, 384], P(('branch', 'seq')), may hold values from -0.09375 to 0.09375
- w_down: bfloat16 [16, 384, 4096], P(('branch', 'seq')), may hold values from -0.21875 to 0.21875
Outputs:
- mixed: bfloat16 [8, 512, 4096], P(('rollout', 'branch'), 'seq'), parts along dimension 0
There are 2 independent parts, one for each index of `rollout`. A program takes and returns all parts, laid end to end along the dimension named above; an argument that names none is the same for every part. Nothing has to cross between parts.
Inputs may be any that keep to these rules, and one draw needn't show every extreme that they name: read_list[c, s, o] is the block of branch c that query block s of branch (c + o + 1) mod 4 reads. `expert_ids`: each token names 2 different experts; of the 128 tokens of one device at most 48 name one expert, and in every draw some expert is named by exactly 48 tokens of some device.
All inputs are finite; a program needn't handle non-finite values.
Results may differ from a plain program's by a relative error of at most 0.0062.
Values may be sent and summed in bfloat16 or wider, within the bound.
A program may use at most 192 MiB of HBM per device.

v0:
```python
import math

import jax
import jax.numpy as jnp
from jax import lax
from jax.sharding import PartitionSpec as P

D = 4096
HEAD_SIZE = 128
QUERY_HEADS = 32
KEY_VALUE_HEADS = 2


def swapped(value, axis, apart):
    mask = 2**apart
    pairs = [(source, source ^ mask) for source in range(lax.axis_size(axis))]
    return lax.ppermute(value, axis, pairs)


def attend_block(q_rows, own_kv, sib_kv, block_index):
    block_len = q_rows.shape[0]
    length_own = own_kv.shape[0]
    positions = block_index * block_len + jnp.arange(block_len, dtype=jnp.int32)
    own_allowed = jnp.arange(length_own, dtype=jnp.int32)[None, :] <= positions[:, None]
    allowed = jnp.concatenate(
        [own_allowed, jnp.ones((block_len, sib_kv.shape[0]), dtype=bool)], axis=1
    )
    key_rows = jnp.concatenate([own_kv[:, 0], sib_kv[:, 0]], axis=0)
    value_rows = jnp.concatenate([own_kv[:, 1], sib_kv[:, 1]], axis=0)
    group_count = QUERY_HEADS // KEY_VALUE_HEADS
    sub_heads = min(group_count, 8)
    inv_scale = 1.0 / math.sqrt(HEAD_SIZE)
    pieces = []
    for head_key_value in range(KEY_VALUE_HEADS):
        key_head = key_rows[:, head_key_value * HEAD_SIZE : (head_key_value + 1) * HEAD_SIZE]
        value_head = value_rows[:, head_key_value * HEAD_SIZE : (head_key_value + 1) * HEAD_SIZE]
        for start_head in range(0, group_count, sub_heads):
            column = (head_key_value * group_count + start_head) * HEAD_SIZE
            query_head = q_rows[:, column : column + sub_heads * HEAD_SIZE].reshape(
                block_len, sub_heads, HEAD_SIZE
            )
            raw_scores = jnp.einsum(
                "tgd,kd->gtk", query_head, key_head, preferred_element_type=jnp.float32
            )
            masked = jnp.where(allowed[None], raw_scores, -1e30)
            row_max = jnp.max(masked, axis=-1, keepdims=True) * inv_scale
            expterm = jnp.exp(masked * inv_scale - row_max)
            probs = (expterm / jnp.sum(expterm, axis=-1, keepdims=True)).astype(jnp.bfloat16)
            mixture = jnp.einsum(
                "gtk,kd->tgd", probs, value_head, preferred_element_type=jnp.float32
            )
            pieces.append(mixture.reshape(block_len, sub_heads * HEAD_SIZE).astype(jnp.bfloat16))
    return jnp.concatenate(pieces, axis=1)


def on_device(queries, keyvals, residual, read_list, router, expert_ids, w_gate_up, w_down):
    block_len = queries.shape[1]
    kv_width = keyvals.shape[-1]
    seq_blocks = lax.axis_size("seq")
    branches = lax.axis_size("branch")
    me_branch = lax.axis_index("branch")
    me_block = lax.axis_index("seq")
    suffix_all = lax.all_gather(keyvals, "seq", axis=1, tiled=True)[0]
    blocks = suffix_all.reshape(seq_blocks, block_len, 2, kv_width)
    picked = blocks[read_list[0, 0]]
    by_offset = jnp.concatenate(
        [jnp.zeros((1, block_len, 2, kv_width), keyvals.dtype), picked], axis=0
    )
    by_dest = (jnp.arange(branches, dtype=jnp.int32) - me_branch) % branches
    outgoing = by_offset[by_dest]
    incoming = lax.all_to_all(outgoing, "branch", split_axis=0, concat_axis=0, tiled=True)
    others = (me_branch + 1 + jnp.arange(branches - 1, dtype=jnp.int32)) % branches
    sibling = incoming[others].reshape((branches - 1) * block_len, 2, kv_width)
    context = attend_block(queries[0], suffix_all, sibling, me_block)
    state = residual[0].astype(jnp.float32) + context.astype(jnp.float32)
    normed = (state * lax.rsqrt(jnp.mean(state * state, axis=-1, keepdims=True) + 1e-06)).astype(
        jnp.bfloat16
    )
    logits = jnp.dot(normed, router, preferred_element_type=jnp.float32)
    routed = expert_ids[0]
    top_count = routed.shape[1]
    experts = router.shape[1]
    chosen_logits = jnp.take_along_axis(logits, routed, axis=1)
    gate_mix = 1.0 / jnp.sum(
        jnp.exp(chosen_logits[:, None, :] - chosen_logits[:, :, None]), axis=-1
    )
    capacity = 2 * ((3 * block_len * top_count + 4 * experts - 1) // (4 * experts))
    half_cap = capacity // 2
    flat_ids = routed.reshape(-1)
    onehot = (flat_ids[:, None] == jnp.arange(experts, dtype=jnp.int32)[None, :]).astype(jnp.int32)
    slot_of = jnp.sum((jnp.cumsum(onehot, axis=0) - 1) * onehot, axis=1)
    row_token = jnp.arange(block_len * top_count, dtype=jnp.int32) // top_count
    sendbuf = (
        jnp.zeros((experts, capacity, D), jnp.bfloat16).at[flat_ids, slot_of].set(normed[row_token])
    )
    pair_half = me_block % 2
    halved = sendbuf.reshape(experts * 2, half_cap, D)
    own_share = lax.all_to_all(halved, ("branch", "seq"), split_axis=0, concat_axis=0, tiled=True)
    theirs = swapped(own_share, "seq", 0)
    rows_in = jnp.where(
        pair_half == 0,
        jnp.concatenate([own_share, theirs], axis=1),
        jnp.concatenate([theirs, own_share], axis=1),
    )
    devices = rows_in.shape[0]
    half_width = D // 2
    expert_rows = rows_in.reshape(devices * capacity, D)
    gate_up = jnp.einsum(
        "rd,dcf->rcf", expert_rows, w_gate_up[0], preferred_element_type=jnp.float32
    )
    hidden_act = (jax.nn.silu(gate_up[:, 0]) * gate_up[:, 1]).astype(jnp.bfloat16)
    down_local = w_down[0]
    kept_cols = lax.dynamic_slice_in_dim(down_local, pair_half * half_width, half_width, 1)
    given_cols = lax.dynamic_slice_in_dim(down_local, (1 - pair_half) * half_width, half_width, 1)
    kept_share = jnp.dot(hidden_act, kept_cols, preferred_element_type=jnp.float32).reshape(
        devices, capacity, half_width
    )
    given_share = jnp.dot(hidden_act, given_cols, preferred_element_type=jnp.float32).reshape(
        devices, capacity, half_width
    )
    gotten = swapped(given_share, "seq", 0)
    finished = (kept_share + gotten).astype(jnp.bfloat16)
    returned = lax.all_to_all(finished, ("branch", "seq"), split_axis=0, concat_axis=0, tiled=True)
    out_table = jnp.swapaxes(returned.reshape(experts, 2, capacity, half_width), 1, 2).reshape(
        experts, capacity, D
    )
    expert_out = out_table[flat_ids, slot_of].reshape(block_len, top_count, D)
    layer_out = state
    for slot_k in range(top_count):
        layer_out = layer_out + gate_mix[:, slot_k : slot_k + 1] * expert_out[:, slot_k].astype(
            jnp.float32
        )
    return layer_out.astype(jnp.bfloat16)[None]


def solution(mesh):
    return jax.shard_map(
        on_device,
        mesh=mesh,
        in_specs=(
            P(("rollout", "branch"), "seq", None),
            P(("rollout", "branch"), "seq", None, None),
            P(("rollout", "branch"), "seq", None),
            P(("rollout", "branch"), "seq", None),
            P(),
            P(("rollout", "branch"), "seq", None),
            P(("branch", "seq"), None, None, None),
            P(("branch", "seq"), None, None),
        ),
        out_specs=P(("rollout", "branch"), "seq", None),
        check_vma=False,
    )
```

profile of v0, /device:TPU:11, one launch (start us, length us, event | category | flops | bytes accessed | tf_op | source)
XLA Modules:
  0.0 366.3 jit_solution(11561085254637891067)
XLA Ops:
  0.0 1.1 copy.62
  1.1 7.7 %all_gather.3 = bf16[1,512,2,256]{3,1,2,0:T(8,128)(2,1)} all-gather(bf16[1,128,2,256]{3,1,2,0:T(8,128)(2,1)S(1)} %copy.62), channel_id=1, replica_groups=mesh['rollout'=2,'branch'=4,'seq'=4] {'seq'}, dimensions={1}, use_global_device_ids=true | all-gather | bytes 655360 | tf_op jit(solution)/shard_map/all_gather | solution.py:63
  9.5 1.6 gather_fusion
  12.0 2.4 gather_fusion.1
  14.4 4.8 %all-to-all-start = ((bf16[4,128,2,256]{3,1,2,0:T(8,128)(2,1)}), bf16[4,128,2,256]{3,1,2,0:T(8,128)(2,1)}, u32[]{:S(2)}, u32[]{:S(2)}) async-start(bf16[4,128,2,256]{3,1,2,0:T(8,128)(2,1)} %gather_fusion.1), calls=%async_computation | async-start | bytes 1048576 | tf_op jit(solution)/shard_map/all_to_all | solution.py:71
  19.7 2.3 copy.64
  23.7 1.8 slice_bitcast_fusion.1
  25.5 2.2 fusion.77
  27.7 2.7 all-to-all-done
  30.4 2.4 gather_fusion.2
  32.8 1.1 copy.63
  33.9 1.7 fusion.38
  36.9 1.5 fusion.2
  38.6 1.0 copy-done.1
  39.5 3.6 fusion.6
  43.2 1.8 fusion.26
  45.0 1.1 copy.82
  46.1 4.0 %fusion.25 = bf16[128,8,128]{2,0,1:T(8,128)(2,1)} fusion(f32[896,128,8]{1,0,2:T(8,128)} %copy-done.3, f32[8,128]{1,0:T(8,128)S(1)} %get-tuple-element.6, f32[8,128]{1,0:T(8,128)S(1)} %get-tuple-element.30, pred[128,896]{0,1:T(8,128)(4,1)} %concatenate.44, bf16[512,256]{1,0:T(8,128)(2,1)} %get-tuple-element.21, bf16[384,256]{1,0:T(8,128)(2,1)} %copy-done.14), kind=kOutput, calls=%fused_computation.52 | convolution fusion | flops 240058368 | bytes 4513792 | tf_op jit(solution)/shard_map/gtk,kd->tgd/dot_general | solution.py:49
  50.1 1.8 copy.83
  51.9 4.0 %fusion.24 = bf16[128,8,128]{2,0,1:T(8,128)(2,1)} fusion(f32[896,128,8]{1,0,2:T(8,128)} %copy-done.2, f32[8,128]{1,0:T(8,128)S(1)} %get-tuple-element.7, f32[8,128]{1,0:T(8,128)S(1)} %get-tuple-element.29, pred[128,896]{0,1:T(8,128)(4,1)} %concatenate.44, bf16[384,256]{1,0:T(8,128)(2,1)} %copy-done.14, bf16[512,256]{1,0:T(8,128)(2,1)} %get-tuple-element.21), kind=kOutput, calls=%fused_computation.51 | convolution fusion | flops 240058368 | bytes 4513792 | tf_op jit(solution)/shard_map/gtk,kd->tgd/dot_general | solution.py:49
  55.9 1.8 copy.84
  57.7 4.0 %fusion.23 = bf16[128,8,128]{2,0,1:T(8,128)(2,1)} fusion(f32[896,128,8]{1,0,2:T(8,128)} %copy-done.1, f32[8,128]{1,0:T(8,128)S(1)} %get-tuple-element.8, f32[8,128]{1,0:T(8,128)S(1)} %get-tuple-element.28, pred[128,896]{0,1:T(8,128)(4,1)} %concatenate.44, bf16[384,256]{1,0:T(8,128)(2,1)} %copy-done.14, bf16[512,256]{1,0:T(8,128)(2,1)} %get-tuple-element.21), kind=kOutput, calls=%fused_computation.50 | convolution fusion | flops 240058368 | bytes 4513792 | tf_op jit(solution)/shard_map/gtk,kd->tgd/dot_general | solution.py:49
  61.7 1.8 copy.85
  63.5 1.8 multiply_reduce_fusion
  65.3 2.8 multiply_convert_fusion
  68.1 6.6 %gather_fusion.3 = bf16[256,4096]{1,0:T(8,128)(2,1)} fusion(bf16[128,4096]{1,0:T(8,128)(2,1)} %multiply_convert_fusion, s32[1024]{0:T(1024)S(1)} %pad_clamp_fusion), kind=kCustom, calls=%fused_computation.3 | custom fusion | bytes 4195328 | tf_op jit(solution)/shard_map/gather | solution.py:94
  74.7 2.0 broadcast_in_dim.33
  76.8 66.6 %scatter_fusion = bf16[8,48,4096]{2,1,0:T(8,128)(2,1)} fusion(bf16[8,48,4096]{2,1,0:T(8,128)(2,1)} %broadcast_in_dim.33, s32[256]{0:T(256)S(1)} %bitcast.187, bf16[256,4096]{1,0:T(8,128)(2,1)} %gather_fusion.3), kind=kCustom, calls=%fused_computation.6 | custom fusion | bytes 6293504 | tf_op jit(solution)/shard_map/scatter | solution.py:94
  143.3 79.0 %all_to_all.15 = bf16[16,24,4096]{2,1,0:T(8,128)(2,1)} all-to-all(bf16[16,24,4096]{2,1,0:T(8,128)(2,1)} %bitcast.184), channel_id=1, replica_groups=mesh['rollout'=2,'branch'=4,'seq'=4] {'branch','seq'}, dimensions={0} | all-to-all | bytes 6291456 | tf_op jit(solution)/shard_map/all_to_all | solution.py:98
  222.5 5.9 %collective-permute-done = bf16[16,24,4096]{2,1,0:T(8,128)(2,1)} collective-permute-done((bf16[16,24,4096]{2,1,0:T(8,128)(2,1)}, bf16[16,24,4096]{2,1,0:T(8,128)(2,1)}, u32[]{:S(2)}, u32[]{:S(2)}) %collective-permute-start) | collective-permute-done | bytes 3145760 | tf_op jit(solution)/shard_map/ppermute | solution.py:17
  228.4 5.8 %maximum_select_fusion = bf16[16,48,4096]{2,1,0:T(8,128)(2,1)S(1)} fusion(bf16[16,24,4096]{2,1,0:T(8,128)(2,1)} %collective-permute-done, bf16[16,24,4096]{2,1,0:T(8,128)(2,1)} %all_to_all.15, pred[]{:T(512)S(6)} %eq.34), kind=kLoop, calls=%fused_computation.7 | loop fusion | flops 28311552 | bytes 12582913 | tf_op jit(solution)/shard_map/jit(_where)/select_n | solution.py:100
  234.2 7.3 %fusion = f32[768,2,384]{2,0,1:T(8,128)S(1)} fusion(bf16[768,4096,1]{1,0,2:T(8,128)(2,1)S(1)} %bitcast.190, bf16[4096,2,384]{2,1,0:T(2,128)(2,1)} %bitcast.209), kind=kOutput, calls=%fused_computation.8 | convolution fusion | flops 4831838208 | bytes 14942208 | tf_op jit(solution)/shard_map/rd,dcf->rcf/dot_general | solution.py:108
  241.8 4.5 %fusion.18 = f32[16,48,2048]{2,1,0:T(8,128)} fusion(bf16[16,48,384]{2,1,0:T(8,128)(2,1)S(1)} %bitcast.188, bf16[1,384,4096]{2,1,0:T(8,128)(2,1)S(1)} %copy-done, s32[]{:T(128)S(6)} %select_n.199), kind=kOutput, calls=%fused_computation.45 | convolution fusion | flops 1207959552 | bytes 8454148 | tf_op jit(solution)/shard_map/dot_general | solution.py:118
  246.5 10.4 %collective-permute-done.1 = f32[16,48,2048]{2,1,0:T(8,128)} collective-permute-done((f32[16,48,2048]{2,1,0:T(8,128)}, f32[16,48,2048]{2,1,0:T(8,128)}, u32[]{:S(2)}, u32[]{:S(2)}) %collective-permute-start.1) | collective-permute-done | bytes 6291488 | tf_op jit(solution)/shard_map/ppermute | solution.py:17
  256.8 6.5 %add_convert_fusion = bf16[16,48,2048]{2,1,0:T(8,128)(2,1)} fusion(f32[16,48,2048]{2,1,0:T(8,128)} %collective-permute-done.1, bf16[16,48,384]{2,1,0:T(8,128)(2,1)} %bitcast.189, bf16[1,384,4096]{2,1,0:T(8,128)(2,1)S(1)} %copy-done, s32[]{:T(128)S(6)} %select_n.198), kind=kOutput, calls=%fused_computation.10 | convolution fusion | flops 1211105280 | bytes 11599876 | tf_op jit(solution)/shard_map/dot_general | solution.py:115
  263.3 5.3 %all-to-all-start.2 = ((bf16[16,48,2048]{2,1,0:T(8,128)(2,1)}), bf16[16,48,2048]{2,1,0:T(8,128)(2,1)}, u32[]{:S(2)}, u32[]{:S(2)}) async-start(bf16[16,48,2048]{2,1,0:T(8,128)(2,1)} %add_convert_fusion), calls=%async_computation.2 | async-start | bytes 6291456 | tf_op jit(solution)/shard_map/all_to_all | solution.py:123
  268.9 1.6 fusion.78
  270.5 1.4 gather_fusion.5
  272.1 1.1 copy.77
  273.3 1.8 copy.78
  275.0 1.8 copy.79
  276.8 1.8 copy.80
  278.7 59.8 %all-to-all-done.2 = bf16[16,48,2048]{2,1,0:T(8,128)(2,1)} async-done(((bf16[16,48,2048]{2,1,0:T(8,128)(2,1)}), bf16[16,48,2048]{2,1,0:T(8,128)(2,1)}, u32[]{:S(2)}, u32[]{:S(2)}) %all-to-all-start.2) | async-done | bytes 3145760 | tf_op jit(solution)/shard_map/all_to_all | solution.py:123
  338.5 4.0 %copy.114 = bf16[8,2,6,8,2048]{4,3,1,2,0:T(8,128)(2,1)} copy(bf16[8,2,6,8,2048]{4,3,2,1,0:T(8,128)(2,1)} %bitcast.75) | data formatting | bytes 6291456 | tf_op jit(solution)/shard_map/reshape | solution.py:124
  342.5 7.5 %gather_fusion.4 = bf16[256,4096]{1,0:T(8,128)(2,1)} fusion(bf16[8,48,4096]{2,1,0:T(8,128)(2,1)} %bitcast.185, s32[256]{0:T(256)S(1)} %bitcast.186), kind=kCustom, calls=%fused_computation.4 | custom fusion | bytes 4196352 | tf_op jit(solution)/shard_map/gather | solution.py:127
  350.0 4.4 %reshape.546 = bf16[128,2,4096]{2,1,0:T(2,128)(2,1)} reshape(bf16[256,4096]{1,0:T(8,128)(2,1)} %gather_fusion.4) | data formatting | bytes 4194304 | tf_op jit(solution)/shard_map/reshape | solution.py:127
  354.4 6.3 %fusion.76 = (bf16[128,1,4096]{2,1,0:T(2,128)(2,1)S(1)}, bf16[128,1,4096]{2,1,0:T(2,128)(2,1)S(1)}) fusion(bf16[128,2,4096]{2,1,0:T(2,128)(2,1)} %reshape.546), kind=kLoop, calls=%fused_computation.149 | loop fusion | bytes 4194304 | tf_op jit(solution)/shard_map/slice | solution.py:130
  360.8 5.2 %fusion.12 = bf16[1,128,4096]{2,1,0:T(8,128)(2,1)} fusion(bf16[1,128,4096]{2,1,0:T(8,128)(2,1)S(1)} %copy-done.4, bf16[1,128,1024]{2,1,0:T(8,128)(2,1)S(1)} %copy-done.9, bf16[1,128,1024]{2,1,0:T(8,128)(2,1)S(1)} %copy-done.8, bf16[1,128,1024]{2,1,0:T(8,128)(2,1)S(1)} %copy-done.7, bf16[1,128,1024]{2,1,0:T(8,128)(2,1)S(1)} %copy.77, ...), kind=kLoop, calls=%fused_computation.35 | loop fusion | flops 8912896 | bytes 5243904 | tf_op jit(solution)/shard_map/convert_element_type | solution.py:133
  (74 shorter events, 6.3 us)
Async XLA Ops:
  0.0 241.8 %copy-start = (bf16[1,384,4096]{2,1,0:T(8,128)(2,1)S(1)}, bf16[1,384,4096]{2,1,0:T(8,128)(2,1)}, u32[]{:S(2)}) copy-start(bf16[1,384,4096]{2,1,0:T(8,128)(2,1)} %param.15) | copy-start | bytes 9437188
  0.0 19.1 %copy-start.16 = (s32[1,128,2]{1,2,0:T(2,128)S(1)}, s32[1,128,2]{1,2,0:T(2,128)}, u32[]{:S(2)}) copy-start(s32[1,128,2]{1,2,0:T(2,128)} %param.13) | copy-start | bytes 3076
  14.4 16.0 %all-to-all-start = ((bf16[4,128,2,256]{3,1,2,0:T(8,128)(2,1)}), bf16[4,128,2,256]{3,1,2,0:T(8,128)(2,1)}, u32[]{:S(2)}, u32[]{:S(2)}) async-start(bf16[4,128,2,256]{3,1,2,0:T(8,128)(2,1)} %gather_fusion.1), calls=%async_computation | async-start | bytes 1048576 | tf_op jit(solution)/shard_map/all_to_all | solution.py:71
  32.8 2.8 copy-start.11
  33.9 9.3 %copy-start.14 = (bf16[384,256]{1,0:T(8,128)(2,1)}, bf16[384,256]{1,0:T(8,128)(2,1)S(1)}, u32[]{:S(2)}) copy-start(bf16[384,256]{1,0:T(8,128)(2,1)S(1)} %get-tuple-element.23) | copy-start | bytes 589828
  33.9 2.4 copy-start.10
  35.5 2.9 copy-start.2
  35.6 1.3 copy-start.6
  35.6 1.3 copy-start.12
  36.2 2.3 copy-start.3
  36.9 2.7 copy-start.1
  39.5 3.6 copy-start.13
  222.4 6.0 %collective-permute-start = (bf16[16,24,4096]{2,1,0:T(8,128)(2,1)}, bf16[16,24,4096]{2,1,0:T(8,128)(2,1)}, u32[]{:S(2)}, u32[]{:S(2)}) collective-permute-start(bf16[16,24,4096]{2,1,0:T(8,128)(2,1)} %all_to_all.15), channel_id=1, source_target_pairs={{0,1},{1,0},{2,3},{3,2},{4,5},{5,4},{6,7},{7,6},{8,9},{9,8},{10,11... | collective-permute-start | bytes 9437192 | tf_op jit(solution)/shard_map/ppermute | solution.py:17
  241.8 4.5 %copy-start.5 = (bf16[768,1,384]{2,0,1:T(8,128)(2,1)}, bf16[768,1,384]{2,0,1:T(8,128)(2,1)S(1)}, u32[]{:S(2)}) copy-start(bf16[768,1,384]{2,0,1:T(8,128)(2,1)S(1)} %fusion.27) | copy-start | bytes 1769476
  246.3 10.5 %collective-permute-start.1 = (f32[16,48,2048]{2,1,0:T(8,128)}, f32[16,48,2048]{2,1,0:T(8,128)}, u32[]{:S(2)}, u32[]{:S(2)}) collective-permute-start(f32[16,48,2048]{2,1,0:T(8,128)} %fusion.18), channel_id=1, source_target_pairs={{0,1},{1,0},{2,3},{3,2},{4,5},{5,4},{6,7},{7,6},{8,9},{9,8},{10,11... | collective-permute-start | bytes 18874376 | tf_op jit(solution)/shard_map/ppermute | solution.py:17
  263.3 5.6 %copy-start.15 = (bf16[4096,8]{0,1:T(8,128)(2,1)S(1)}, bf16[4096,8]{0,1:T(8,128)(2,1)}, u32[]{:S(2)}) copy-start(bf16[4096,8]{0,1:T(8,128)(2,1)} %param.12) | copy-start | bytes 196612
  263.3 75.2 %all-to-all-start.2 = ((bf16[16,48,2048]{2,1,0:T(8,128)(2,1)}), bf16[16,48,2048]{2,1,0:T(8,128)(2,1)}, u32[]{:S(2)}, u32[]{:S(2)}) async-start(bf16[16,48,2048]{2,1,0:T(8,128)(2,1)} %add_convert_fusion), calls=%async_computation.2 | async-start | bytes 6291456 | tf_op jit(solution)/shard_map/all_to_all | solution.py:123
  354.4 6.3 %copy-start.4 = (bf16[1,128,4096]{2,1,0:T(8,128)(2,1)S(1)}, bf16[1,128,4096]{2,1,0:T(8,128)(2,1)}, u32[]{:S(2)}) copy-start(bf16[1,128,4096]{2,1,0:T(8,128)(2,1)} %param.10) | copy-start | bytes 3145732
  354.4 6.3 %copy-start.7 = (bf16[1,128,1024]{2,1,0:T(8,128)(2,1)S(1)}, bf16[1,128,1024]{2,1,0:T(8,128)(2,1)}, u32[]{:S(2)}) copy-start(bf16[1,128,1024]{2,1,0:T(8,128)(2,1)} %copy.78) | copy-start | bytes 786436
  354.4 6.3 %copy-start.8 = (bf16[1,128,1024]{2,1,0:T(8,128)(2,1)S(1)}, bf16[1,128,1024]{2,1,0:T(8,128)(2,1)}, u32[]{:S(2)}) copy-start(bf16[1,128,1024]{2,1,0:T(8,128)(2,1)} %copy.79) | copy-start | bytes 786436
  354.4 6.3 %copy-start.9 = (bf16[1,128,1024]{2,1,0:T(8,128)(2,1)S(1)}, bf16[1,128,1024]{2,1,0:T(8,128)(2,1)}, u32[]{:S(2)}) copy-start(bf16[1,128,1024]{2,1,0:T(8,128)(2,1)} %copy.80) | copy-start | bytes 786436
where the time goes:
time: 373 us; the launch traced here: 366 us
  local copies, waits for them, and re-layouts  130 us (35%)
  blocking collectives  86.7 us (23%)
  waiting for transfers between devices  78.8 us (21%)
  matrix products  38.1 us (10%)
  other arithmetic  21.2 us (6%)
  starting transfers between devices  10.4 us (3%)
    all_to_all x1, blocking collectives, on_device(): lax.all_to_all(halved, ('branch', 'seq'), split_axis=0, concat_axis=0, ti...  79 us
    scatter x1, local copies, waits for them, and re-layouts, on_device(): jnp.zeros((experts, capacity, D), jnp.bfloat16).at[flat_ids, slot_of]  66.6 us
    all_to_all x1, waiting for transfers between devices, on_device(): lax.all_to_all(finished, ('branch', 'seq'), split_axis=0, concat_axis=0,...  59.8 us
    ppermute x2, waiting for transfers between devices, swapped(): return lax.ppermute(value, axis, pairs)  16.2 us
    dot_general x4, matrix products, attend_block(): jnp.einsum('gtk,kd->tgd', probs, value_head, preferred_element_type=jnp.f...  13.8 us
    all_gather x1, blocking collectives, on_device(): suffix_all = lax.all_gather(keyvals, 'seq', axis=1, tiled=True)[0]  7.73 us
    gather x1, local copies, waits for them, and re-layouts, on_device(): expert_out = out_table[flat_ids, slot_of].reshape(block_len, top_count, D)  7.52 us
  transfers between devices with their start and end apart: 4, of which 4 were waited for; matrix products, arithmetic and copies ran while one was open for 5% of the time, Pallas kernels for 0%

commit v1 on v0

v1 whole, which is shorter than its diff:
```python
import functools
import math

import jax
import jax.numpy as jnp
from jax import lax
from jax.experimental import pallas as pl
from jax.experimental.pallas import tpu as pltpu
from jax.sharding import PartitionSpec as P

HEAD_SIZE = 128
VMEM_LIMIT = 60 * 1024 * 1024
F32 = jnp.float32
BF16 = jnp.bfloat16
ANY = pl.BlockSpec(memory_space=pl.ANY)
VMEM = pl.BlockSpec(memory_space=pltpu.VMEM)
SMEM = pl.BlockSpec(memory_space=pltpu.SMEM)


def flipped(number, mask, count):
    value, bit = 0, 1
    while bit < count:
        value = value + ((number // bit + mask // bit) % 2) * bit
        bit *= 2
    return value


def kv_kernel(n_branch, n_seq, list_ref, kv_ref, own_ref, sib_ref, picked, s1, r1, s2, r2, lsem):
    branch = lax.axis_index("branch")
    seq = lax.axis_index("seq")
    barrier = pltpu.get_barrier_semaphore()
    for step in range(1, n_seq):
        pl.semaphore_signal(
            barrier, inc=1, device_id={"seq": (seq + step) % n_seq},
            device_id_type=pl.DeviceIdType.MESH,
        )
    for step in range(1, n_branch):
        pl.semaphore_signal(
            barrier, inc=1, device_id={"branch": (branch + step) % n_branch},
            device_id_type=pl.DeviceIdType.MESH,
        )
    pl.semaphore_wait(barrier, n_seq - 1 + n_branch - 1)
    mine = pltpu.make_async_copy(kv_ref, own_ref.at[seq], lsem)
    mine.start()
    first = []
    for step in range(1, n_seq):
        copy = pltpu.make_async_remote_copy(
            src_ref=kv_ref, dst_ref=own_ref.at[seq],
            send_sem=s1.at[step], recv_sem=r1.at[step],
            device_id={"seq": (seq + step) % n_seq}, device_id_type=pl.DeviceIdType.MESH,
        )
        copy.start()
        first.append(copy)
    mine.wait()
    for copy in first:
        copy.wait()
    second = []
    for offset in range(n_branch - 1):
        picked[offset] = own_ref[list_ref[offset]]
    for offset in range(n_branch - 1):
        copy = pltpu.make_async_remote_copy(
            src_ref=picked.at[offset], dst_ref=sib_ref.at[offset],
            send_sem=s2.at[offset], recv_sem=r2.at[offset],
            device_id={"branch": (branch + offset + 1) % n_branch},
            device_id_type=pl.DeviceIdType.MESH,
        )
        copy.start()
        second.append(copy)
    for copy in second:
        copy.wait()


def exchange_kv(kv, listed, n_branch, n_seq):
    rows, width = kv.shape
    return pl.pallas_call(
        functools.partial(kv_kernel, n_branch, n_seq),
        out_shape=(
            jax.ShapeDtypeStruct((n_seq, rows, width), BF16),
            jax.ShapeDtypeStruct((n_branch - 1, rows, width), BF16),
        ),
        in_specs=[SMEM, VMEM],
        out_specs=(VMEM, VMEM),
        scratch_shapes=[
            pltpu.VMEM((n_branch - 1, rows, width), BF16),
            pltpu.SemaphoreType.DMA((n_seq,)),
            pltpu.SemaphoreType.DMA((n_seq,)),
            pltpu.SemaphoreType.DMA((n_branch,)),
            pltpu.SemaphoreType.DMA((n_branch,)),
            pltpu.SemaphoreType.DMA,
        ],
        compiler_params=pltpu.CompilerParams(
            collective_id=0, has_side_effects=True, vmem_limit_bytes=VMEM_LIMIT
        ),
    )(listed, kv)


def attend_kernel(
    experts, cap, n_seq,
    q_ref, own_ref, sib_ref, res_ref, router_ref, ids_ref, idt_ref,
    send_ref, state_ref, gate_ref,
):
    seq = lax.axis_index("seq")
    me = (lax.axis_index("branch") * n_seq + seq) // 2
    rows, width = q_ref.shape
    kv_heads = own_ref.shape[1] // (2 * HEAD_SIZE)
    group = width // HEAD_SIZE // kv_heads
    together = 2
    own_len = own_ref.shape[0]
    scale = 1.0 / math.sqrt(HEAD_SIZE)
    nt = (((1,), (1,)), ((), ()))
    where = seq * rows + lax.broadcasted_iota(jnp.int32, (together * rows, own_len), 0) % rows
    bias = jnp.where(
        lax.broadcasted_iota(jnp.int32, (together * rows, own_len), 1) <= where, 0.0, -1e30
    )
    for head in range(kv_heads):
        kcol = slice(head * HEAD_SIZE, (head + 1) * HEAD_SIZE)
        vcol = slice((kv_heads + head) * HEAD_SIZE, (kv_heads + head + 1) * HEAD_SIZE)

        @pl.loop(0, group // together)
        def _(step):
            base = (head * group + step * together) * HEAD_SIZE
            cols = [
                pl.ds(pl.multiple_of(base + i * HEAD_SIZE, HEAD_SIZE), HEAD_SIZE)
                for i in range(together)
            ]
            q = jnp.concatenate([q_ref[:, c] for c in cols], axis=0)
            s_own = lax.dot_general(q, own_ref[:, kcol], nt, preferred_element_type=F32)
            s_sib = lax.dot_general(q, sib_ref[:, kcol], nt, preferred_element_type=F32)
            s_own = s_own * scale + bias
            s_sib = s_sib * scale
            top = jnp.maximum(
                jnp.max(s_own, axis=1, keepdims=True), jnp.max(s_sib, axis=1, keepdims=True)
            )
            p_own = jnp.exp(s_own - top)
            p_sib = jnp.exp(s_sib - top)
            total = jnp.sum(p_own, axis=1, keepdims=True) + jnp.sum(p_sib, axis=1, keepdims=True)
            mixed = jnp.dot(p_own.astype(BF16), own_ref[:, vcol], preferred_element_type=F32)
            mixed += jnp.dot(p_sib.astype(BF16), sib_ref[:, vcol], preferred_element_type=F32)
            mixed = (mixed / total).astype(BF16).astype(F32)
            for i, c in enumerate(cols):
                state_ref[:, c] = res_ref[:, c].astype(F32) + mixed[i * rows : (i + 1) * rows]

    state = state_ref[...]
    normed = (
        state * lax.rsqrt(jnp.mean(state * state, axis=1, keepdims=True) + 1e-06)
    ).astype(BF16)
    logits = lax.dot_general(normed, router_ref[...], nt, preferred_element_type=F32)

    top_count = ids_ref.shape[1]
    ids, idt = ids_ref[...], idt_ref[...]
    kinds = lax.broadcasted_iota(jnp.int32, (rows, experts), 1)
    kinds_t = lax.broadcasted_iota(jnp.int32, (experts, rows), 0)
    hot = [(ids[:, k : k + 1] == kinds).astype(F32) for k in range(top_count)]
    hot_t = [(idt[k : k + 1, :] == kinds_t).astype(F32) for k in range(top_count)]
    down = lax.broadcasted_iota(jnp.int32, (rows, rows), 0)
    along = lax.broadcasted_iota(jnp.int32, (rows, rows), 1)
    before = jnp.dot((along < down).astype(F32).astype(BF16), sum(hot).astype(BF16), preferred_element_type=F32)
    before_t = jnp.dot(sum(hot_t).astype(BF16), (down < along).astype(F32).astype(BF16), preferred_element_type=F32)
    dest, dest_t = [], []
    for k in range(top_count):
        slot = jnp.sum(before * hot[k], axis=1, keepdims=True).astype(jnp.int32)
        dest.append((ids[:, k : k + 1] ^ me) * cap + slot)
        slot_t = jnp.sum(before_t * hot_t[k], axis=0, keepdims=True).astype(jnp.int32)
        dest_t.append((idt[k : k + 1, :] ^ me) * cap + slot_t)
    chosen = [jnp.sum(logits * hot[k], axis=1, keepdims=True) for k in range(top_count)]
    gates = [1.0 / sum(jnp.exp(c - chosen[k]) for c in chosen) for k in range(top_count)]

    pair = 2 * cap
    places = lax.broadcasted_iota(jnp.int32, (rows, pair), 1)
    places_t = lax.broadcasted_iota(jnp.int32, (pair, rows), 0)
    for p in range(experts // 2):
        pick = sum((dest_t[k] - p * pair == places_t).astype(F32) for k in range(top_count))
        send_ref[p * pair : (p + 1) * pair, :] = jnp.dot(
            pick.astype(BF16), normed, preferred_element_type=F32
        ).astype(BF16)
        weight = sum(
            jnp.where(dest[k] - p * pair == places, gates[k], 0.0) for k in range(top_count)
        )
        high = weight.astype(BF16)
        gate_ref[p, 0] = high
        gate_ref[p, 1] = (weight - high.astype(F32)).astype(BF16)


def attend(q, own, sib, residual, router_t, ids, experts, cap, n_seq):
    rows, width = q.shape
    return pl.pallas_call(
        functools.partial(attend_kernel, experts, cap, n_seq),
        out_shape=(
            jax.ShapeDtypeStruct((experts * cap, width), BF16),
            jax.ShapeDtypeStruct((rows, width), F32),
            jax.ShapeDtypeStruct((experts // 2, 2, rows, 2 * cap), BF16),
        ),
        in_specs=[VMEM] * 7,
        out_specs=(VMEM, VMEM, VMEM),
        compiler_params=pltpu.CompilerParams(vmem_limit_bytes=VMEM_LIMIT),
    )(q, own, sib, residual, router_t, ids, ids.T)


def expert_kernel(
    experts, cap, n_seq,
    send_ref, state_ref, gate_ref, wgu_ref, wdn_ref, out_ref,
    recv, res, ret, wgu, wdn, acc,
    wsend, wrecv, wloc, lsem, dsend, drecv, bsend, brecv,
):
    branch = lax.axis_index("branch")
    seq = lax.axis_index("seq")
    core = seq % 2
    me = (branch * n_seq + seq) // 2
    pair = 2 * cap
    width = send_ref.shape[1]
    twin = {"seq": seq + 1 - 2 * core}
    mesh_id = pl.DeviceIdType.MESH

    def place(k):
        other = flipped(me, k, experts)
        return {"branch": (2 * other) // n_seq, "seq": (2 * other) % n_seq + core}

    barrier = pltpu.get_barrier_semaphore()
    pl.semaphore_signal(barrier, inc=1, device_id=twin, device_id_type=mesh_id)

    @pl.loop(1, experts)
    def _(k):
        pl.semaphore_signal(barrier, inc=1, device_id=place(k), device_id_type=mesh_id)

    pl.semaphore_wait(barrier, experts)

    def block(k):
        return pl.ds(pl.multiple_of(k * cap, 16), cap)

    def dispatch(k):
        return pltpu.make_async_remote_copy(
            src_ref=send_ref.at[block(k)], dst_ref=recv.at[block(k)],
            send_sem=dsend.at[k], recv_sem=drecv.at[k],
            device_id=place(k), device_id_type=mesh_id,
        )

    def give_back(k):
        return pltpu.make_async_remote_copy(
            src_ref=res.at[block(k)], dst_ref=ret.at[block(k)],
            send_sem=bsend.at[k], recv_sem=brecv.at[k],
            device_id=place(k), device_id_type=mesh_id,
        )

    weights = []
    for i, (src, dst) in enumerate(((wgu_ref, wgu), (wdn_ref, wdn))):
        weights.append(
            pltpu.make_async_remote_copy(
                src_ref=src, dst_ref=dst.at[1], send_sem=wsend.at[i], recv_sem=wrecv.at[i],
                device_id=twin, device_id_type=mesh_id,
            )
        )
        weights.append(pltpu.make_async_copy(src, dst.at[0], wloc.at[i]))
    dispatch(1).start()
    mine = pltpu.make_async_copy(send_ref.at[block(0)], recv.at[block(0)], lsem)
    mine.start()

    @pl.loop(experts // 2, experts)
    def _(k):
        dispatch(k).start()

    @pl.loop(2, experts // 2)
    def _(k):
        dispatch(k).start()

    for copy in weights:
        copy.start()
    acc[...] = state_ref[...]
    for copy in weights:
        copy.wait()

    chunk = 512

    def compute(p):
        span = pl.ds(pl.multiple_of(p * pair, 16), pair)
        acts = []
        for h in range(2):
            x = recv[span, :]
            gate = jnp.dot(x, wgu[h, 0], preferred_element_type=F32)
            up = jnp.dot(x, wgu[h, 1], preferred_element_type=F32)
            acts.append((gate / (1.0 + jnp.exp(-gate)) * up).astype(BF16))
        for start in range(0, width, chunk):
            cols = slice(start, start + chunk)
            done = jnp.dot(acts[0], wdn[0, :, cols], preferred_element_type=F32)
            done += jnp.dot(acts[1], wdn[1, :, cols], preferred_element_type=F32)
            res[span, cols] = done.astype(BF16)

    quarter = experts // 4

    def turn(i):
        return jnp.where(i <= quarter, i + quarter - 1, i - quarter)

    mine.wait()
    dispatch(1).wait_recv()
    compute(0)
    give_back(1).start()

    @pl.loop(1, experts // 2)
    def _(i):
        p = turn(i)
        dispatch(2 * p).wait_recv()
        dispatch(2 * p + 1).wait_recv()
        compute(p)
        give_back(2 * p).start()
        give_back(2 * p + 1).start()

    def add(p, rows):
        for start in range(0, width, chunk):
            cols = slice(start, start + chunk)
            block_rows = rows(cols)
            acc[:, cols] += jnp.dot(
                gate_ref[p, 0], block_rows, preferred_element_type=F32
            ) + jnp.dot(gate_ref[p, 1], block_rows, preferred_element_type=F32)

    give_back(1).wait_recv()
    add(0, lambda cols: jnp.concatenate([res[0:cap, cols], ret[cap:pair, cols]], axis=0))

    @pl.loop(1, experts // 2)
    def _(i):
        p = turn(i)
        give_back(2 * p).wait_recv()
        give_back(2 * p + 1).wait_recv()
        span = pl.ds(pl.multiple_of(p * pair, 16), pair)
        add(p, lambda cols: ret[span, cols])

    out_ref[...] = acc[...].astype(BF16)

    @pl.loop(1, experts)
    def _(k):
        dispatch(k).wait_send()
        give_back(k).wait_send()


def run_experts(send, state, gate, wgu, wdn, experts, cap, n_seq):
    rows, width = state.shape
    ff = wdn.shape[0]
    return pl.pallas_call(
        functools.partial(expert_kernel, experts, cap, n_seq),
        out_shape=jax.ShapeDtypeStruct((rows, width), BF16),
        in_specs=[ANY, VMEM, VMEM, ANY, ANY],
        out_specs=VMEM,
        scratch_shapes=[
            pltpu.VMEM((experts * cap, width), BF16),
            pltpu.VMEM((experts * cap, width), BF16),
            pltpu.VMEM((experts * cap, width), BF16),
            pltpu.VMEM((2, 2, width, ff), BF16),
            pltpu.VMEM((2, ff, width), BF16),
            pltpu.VMEM((rows, width), F32),
            pltpu.SemaphoreType.DMA((2,)),
            pltpu.SemaphoreType.DMA((2,)),
            pltpu.SemaphoreType.DMA((2,)),
            pltpu.SemaphoreType.DMA,
            pltpu.SemaphoreType.DMA((experts,)),
            pltpu.SemaphoreType.DMA((experts,)),
            pltpu.SemaphoreType.DMA((experts,)),
            pltpu.SemaphoreType.DMA((experts,)),
        ],
        compiler_params=pltpu.CompilerParams(
            collective_id=1, has_side_effects=True, vmem_limit_bytes=VMEM_LIMIT
        ),
    )(send, state, gate, wgu, wdn)


def on_device(
    n_branch, n_seq, queries, keyvals, residual, read_list, router, expert_ids, w_gate_up, w_down
):
    rows = queries.shape[1]
    experts = router.shape[1]
    top_count = expert_ids.shape[2]
    capacity = 2 * ((3 * rows * top_count + 4 * experts - 1) // (4 * experts))
    cap = (capacity + 15) // 16 * 16
    kv = keyvals.reshape(rows, -1)
    own, sib = exchange_kv(kv, read_list.reshape(-1), n_branch, n_seq)
    own = own.reshape(-1, kv.shape[1])
    sib = sib.reshape(-1, kv.shape[1])
    wgu = jnp.swapaxes(w_gate_up[0], 0, 1)
    send, state, gate = attend(
        queries[0], own, sib, residual[0], router.T, expert_ids[0], experts, cap, n_seq
    )
    return run_experts(send, state, gate, wgu, w_down[0], experts, cap, n_seq)[None]


def solution(mesh):
    return jax.shard_map(
        functools.partial(on_device, mesh.shape["branch"], mesh.shape["seq"]),
        mesh=mesh,
        in_specs=(
            P(("rollout", "branch"), "seq", None),
            P(("rollout", "branch"), "seq", None, None),
            P(("rollout", "branch"), "seq", None),
            P(("rollout", "branch"), "seq", None),
            P(),
            P(("rollout", "branch"), "seq", None),
            P(("branch", "seq"), None, None, None),
            P(("branch", "seq"), None, None),
        ),
        out_specs=P(("rollout", "branch"), "seq", None),
        check_vma=False,
    )
```

time: 373 us -> 198 us (0.53)
  the two profiles are of different devices: /device:TPU:11 before, /device:TPU:0 now
where the time goes in v1:
time: 198 us; the launch traced here: 197 us
  Pallas kernels  186 us (94%)
  local copies, waits for them, and re-layouts  11.5 us (6%)
    pallas_call x1, Pallas kernels, run_experts(): pl.pallas_call(functools.partial(expert_kernel, experts, cap, n_seq), out...  147 us
    pallas_call x1, Pallas kernels, exchange_kv(): pl.pallas_call(functools.partial(kv_kernel, n_branch, n_seq), out_shape=(...  23.2 us
    pallas_call x1, Pallas kernels, attend(): pl.pallas_call(functools.partial(attend_kernel, experts, cap, n_seq), out...  15.6 us
    unnamed x3, local copies, waits for them, and re-layouts  10.1 us

profile of v1, /device:TPU:0, one launch (start us, length us, event | category | flops | bytes accessed | tf_op | source)
XLA Modules:
  0.0 197.5 jit_solution(14476736279514501916)
XLA Ops:
  0.0 1.4 copy.9.ids_ref
  1.4 1.6 copy.11
  3.0 23.2 %shard_map.82 = (bf16[4,128,512]{2,1,0:T(8,128)(2,1)}, bf16[3,128,512]{2,1,0:T(8,128)(2,1)}) custom-call(s32[3]{0:T(128)} %bitcast.31, bf16[128,512]{1,0:T(8,128)(2,1)} %bitcast.24), custom_call_target="tpu_custom_call" | custom-call | tf_op jit(solution)/shard_map/pallas_call | solution.py:75
  26.2 15.6 %shard_map.83 = (bf16[384,4096]{1,0:T(8,128)(2,1)}, f32[128,4096]{1,0:T(8,128)}, bf16[4,2,128,96]{3,2,1,0:T(8,128)(2,1)}) custom-call(bf16[128,4096]{1,0:T(8,128)(2,1)} %bitcast.22, bf16[512,512]{1,0:T(8,128)(2,1)} %bitcast.25, bf16[384,512]{1,0:T(8,128)(2,1)} %bitcast.26, bf16[128,4096]{1,0:T(8,128)(2,1)} %bitcast.23, bf16[8,4096]{1,0:T(8,128)(2,1)} %bitcast.28, ...), custom_call_target="tpu_custom_call" | custom-call | tf_op jit(solution)/shard_map/pallas_call | solution.py:186
  41.9 6.2 %copy.13 = bf16[1,4096,2,384]{3,1,2,0:T(8,128)(2,1)} copy(bf16[1,4096,2,384]{3,2,1,0:T(2,128)(2,1)} %param.14) | data formatting | bytes 12582912 | tf_op args[6]
  48.1 147.1 %shard_map.84 = bf16[128,4096]{1,0:T(8,128)(2,1)} custom-call(bf16[384,4096]{1,0:T(8,128)(2,1)} %get-tuple-element.12.send_ref, f32[128,4096]{1,0:T(8,128)} %get-tuple-element.13.state_ref, bf16[4,2,128,96]{3,2,1,0:T(8,128)(2,1)} %get-tuple-element.14.gate_ref, bf16[2,4096,384]{2,1,0:T(8,128)(2,1)} %bitcast.19, bf16[384,4096]{1,0:T(8,128)(2,1)} %bitcast.21), custom_call_target="tpu_custom_call" | custom-call | tf_op jit(solution)/shard_map/pallas_call | solution.py:336
  195.2 2.3 %copy.15 = bf16[1,128,4096]{2,1,0:T(8,128)(2,1)} copy(bf16[1,128,4096]{2,1,0:T(8,128)(2,1)} %bitcast.20) | data formatting | bytes 2097152

commit v2 on v1

--- a/solution.py
+++ b/solution.py
@@ -25,120 +25,108 @@
     return value
 
 
-def kv_kernel(n_branch, n_seq, list_ref, kv_ref, own_ref, sib_ref, picked, s1, r1, s2, r2, lsem):
+def attend_kernel(
+    experts, cap, n_branch, n_seq,
+    list_ref, q_ref, own_ref, res_ref, router_ref, ids_ref, idt_ref,
+    send_ref, state_ref, gate_ref,
+    picked, sib_ref, tops, totals, ssem, rsem,
+):
     branch = lax.axis_index("branch")
     seq = lax.axis_index("seq")
+    me = (branch * n_seq + seq) // 2
+    rows, width = q_ref.shape
+    kv_heads = own_ref.shape[2] // (2 * HEAD_SIZE)
+    group = width // HEAD_SIZE // kv_heads
+    together = 2
+    tall = together * rows
+    own_len = n_seq * rows
+    sib_len = (n_branch - 1) * rows
+    scale = 1.0 / math.sqrt(HEAD_SIZE)
+    nt = (((1,), (1,)), ((), ()))
+
     barrier = pltpu.get_barrier_semaphore()
-    for step in range(1, n_seq):
-        pl.semaphore_signal(
-            barrier, inc=1, device_id={"seq": (seq + step) % n_seq},
-            device_id_type=pl.DeviceIdType.MESH,
-        )
     for step in range(1, n_branch):
         pl.semaphore_signal(
             barrier, inc=1, device_id={"branch": (branch + step) % n_branch},
             device_id_type=pl.DeviceIdType.MESH,
         )
-    pl.semaphore_wait(barrier, n_seq - 1 + n_branch - 1)
-    mine = pltpu.make_async_copy(kv_ref, own_ref.at[seq], lsem)
-    mine.start()
-    first = []
-    for step in range(1, n_seq):
-        copy = pltpu.make_async_remote_copy(
-            src_ref=kv_ref, dst_ref=own_ref.at[seq],
-            send_sem=s1.at[step], recv_sem=r1.at[step],
-            device_id={"seq": (seq + step) % n_seq}, device_id_type=pl.DeviceIdType.MESH,
-        )
-        copy.start()
-        first.append(copy)
-    mine.wait()
-    for copy in first:
-        copy.wait()
-    second = []
     for offset in range(n_branch - 1):
-        picked[offset] = own_ref[list_ref[offset]]
+        picked[offset] = own_ref[(seq - list_ref[offset] + n_seq) % n_seq]
+    pl.semaphore_wait(barrier, n_branch - 1)
+    copies = []
     for offset in range(n_branch - 1):
         copy = pltpu.make_async_remote_copy(
             src_ref=picked.at[offset], dst_ref=sib_ref.at[offset],
-            send_sem=s2.at[offset], recv_sem=r2.at[offset],
+            send_sem=ssem.at[offset], recv_sem=rsem.at[offset],
             device_id={"branch": (branch + offset + 1) % n_branch},
             device_id_type=pl.DeviceIdType.MESH,
         )
         copy.start()
-        second.append(copy)
-    for copy in second:
+        copies.append(copy)
+
+    at_row = lax.broadcasted_iota(jnp.int32, (tall, own_len), 0) % rows
+    at_col = lax.broadcasted_iota(jnp.int32, (tall, own_len), 1)
+    earlier = at_col // rows
+    bias = jnp.where(
+        earlier == 0,
+        jnp.where(at_col <= at_row, 0.0, -1e30),
+        jnp.where(earlier <= seq, 0.0, -1e30),
+    )
+
+    def head_parts(head, step):
+        base = (head * group + step * together) * HEAD_SIZE
+        cols = [
+            pl.ds(pl.multiple_of(base + i * HEAD_SIZE, HEAD_SIZE), HEAD_SIZE)
+            for i in range(together)
+        ]
+        return cols, jnp.concatenate([q_ref[:, c] for c in cols], axis=0)
+
+    def kv_cols(head):
+        return (
+            slice(head * HEAD_SIZE, (head + 1) * HEAD_SIZE),
+            slice((kv_heads + head) * HEAD_SIZE, (kv_heads + head + 1) * HEAD_SIZE),
+        )
+
+    steps = group // together
+    for head in range(kv_heads):
+        kcol, vcol = kv_cols(head)
+
+        @pl.loop(0, steps)
+        def _(step):
+            cols, q = head_parts(head, step)
+            keys = own_ref[:, :, kcol].reshape(own_len, HEAD_SIZE)
+            values = own_ref[:, :, vcol].reshape(own_len, HEAD_SIZE)
+            scores = lax.dot_general(q, keys, nt, preferred_element_type=F32) * scale + bias
+            top = jnp.max(scores, axis=1, keepdims=True)
+            p = jnp.exp(scores - top)
+            tops[head * steps + step] = top
+            totals[head * steps + step] = jnp.sum(p, axis=1, keepdims=True)
+            mixed = jnp.dot(p.astype(BF16), values, preferred_element_type=F32)
+            for i, c in enumerate(cols):
+                state_ref[:, c] = mixed[i * rows : (i + 1) * rows]
+
+    for copy in copies:
         copy.wait()
-
-
-def exchange_kv(kv, listed, n_branch, n_seq):
-    rows, width = kv.shape
-    return pl.pallas_call(
-        functools.partial(kv_kernel, n_branch, n_seq),
-        out_shape=(
-            jax.ShapeDtypeStruct((n_seq, rows, width), BF16),
-            jax.ShapeDtypeStruct((n_branch - 1, rows, width), BF16),
-        ),
-        in_specs=[SMEM, VMEM],
-        out_specs=(VMEM, VMEM),
-        scratch_shapes=[
-            pltpu.VMEM((n_branch - 1, rows, width), BF16),
-            pltpu.SemaphoreType.DMA((n_seq,)),
-            pltpu.SemaphoreType.DMA((n_seq,)),
-            pltpu.SemaphoreType.DMA((n_branch,)),
-            pltpu.SemaphoreType.DMA((n_branch,)),
-            pltpu.SemaphoreType.DMA,
-        ],
-        compiler_params=pltpu.CompilerParams(
-            collective_id=0, has_side_effects=True, vmem_limit_bytes=VMEM_LIMIT
-        ),
-    )(listed, kv)
-
-
-def attend_kernel(
-    experts, cap, n_seq,
-    q_ref, own_ref, sib_ref, res_ref, router_ref, ids_ref, idt_ref,
-    send_ref, state_ref, gate_ref,
-):
-    seq = lax.axis_index("seq")
-    me = (lax.axis_index("branch") * n_seq + seq) // 2
-    rows, width = q_ref.shape
-    kv_heads = own_ref.shape[1] // (2 * HEAD_SIZE)
-    group = width // HEAD_SIZE // kv_heads
-    together = 2
-    own_len = own_ref.shape[0]
-    scale = 1.0 / math.sqrt(HEAD_SIZE)
-    nt = (((1,), (1,)), ((), ()))
-    where = seq * rows + lax.broadcasted_iota(jnp.int32, (together * rows, own_len), 0) % rows
-    bias = jnp.where(
-        lax.broadcasted_iota(jnp.int32, (together * rows, own_len), 1) <= where, 0.0, -1e30
-    )
     for head in range(kv_heads):
-        kcol = slice(head * HEAD_SIZE, (head + 1) * HEAD_SIZE)
-        vcol = slice((kv_heads + head) * HEAD_SIZE, (kv_heads + head + 1) * HEAD_SIZE)
-
-        @pl.loop(0, group // together)
+        kcol, vcol = kv_cols(head)
+
+        @pl.loop(0, steps)
         def _(step):
-            base = (head * group + step * together) * HEAD_SIZE
-            cols = [
-                pl.ds(pl.multiple_of(base + i * HEAD_SIZE, HEAD_SIZE), HEAD_SIZE)
-                for i in range(together)
-            ]
-            q = jnp.concatenate([q_ref[:, c] for c in cols], axis=0)
-            s_own = lax.dot_general(q, own_ref[:, kcol], nt, preferred_element_type=F32)
-            s_sib = lax.dot_general(q, sib_ref[:, kcol], nt, preferred_element_type=F32)
-            s_own = s_own * scale + bias
-            s_sib = s_sib * scale
-            top = jnp.maximum(
-                jnp.max(s_own, axis=1, keepdims=True), jnp.max(s_sib, axis=1, keepdims=True)
-            )
-            p_own = jnp.exp(s_own - top)
-            p_sib = jnp.exp(s_sib - top)
-            total = jnp.sum(p_own, axis=1, keepdims=True) + jnp.sum(p_sib, axis=1, keepdims=True)
-            mixed = jnp.dot(p_own.astype(BF16), own_ref[:, vcol], preferred_element_type=F32)
-            mixed += jnp.dot(p_sib.astype(BF16), sib_ref[:, vcol], preferred_element_type=F32)
-            mixed = (mixed / total).astype(BF16).astype(F32)
+            cols, q = head_parts(head, step)
+            keys = sib_ref[:, :, kcol].reshape(sib_len, HEAD_SIZE)
+            values = sib_ref[:, :, vcol].reshape(sib_len, HEAD_SIZE)
+            scores = lax.dot_general(q, keys, nt, preferred_element_type=F32) * scale
+            own_top = tops[head * steps + step]
+            top = jnp.maximum(own_top, jnp.max(scores, axis=1, keepdims=True))
+            p = jnp.exp(scores - top)
+            shrink = jnp.exp(own_top - top)
+            total = totals[head * steps + step] * shrink + jnp.sum(p, axis=1, keepdims=True)
+            mixed = jnp.dot(p.astype(BF16), values, preferred_element_type=F32)
+            inverse = 1.0 / total
             for i, c in enumerate(cols):
-                state_ref[:, c] = res_ref[:, c].astype(F32) + mixed[i * rows : (i + 1) * rows]
+                part = slice(i * rows, (i + 1) * rows)
+                context = (state_ref[:, c] * shrink[part] + mixed[part]) * inverse[part]
+                state_ref[:, c] = res_ref[:, c].astype(F32) + context.astype(BF16).astype(F32)
 
     state = state_ref[...]
     normed = (
@@ -181,19 +169,30 @@
         gate_ref[p, 1] = (weight - high.astype(F32)).astype(BF16)
 
 
-def attend(q, own, sib, residual, router_t, ids, experts, cap, n_seq):
+def attend(listed, q, own, residual, router_t, ids, experts, cap, n_branch, n_seq):
     rows, width = q.shape
+    halves = width // HEAD_SIZE // 2
     return pl.pallas_call(
-        functools.partial(attend_kernel, experts, cap, n_seq),
+        functools.partial(attend_kernel, experts, cap, n_branch, n_seq),
         out_shape=(
             jax.ShapeDtypeStruct((experts * cap, width), BF16),
             jax.ShapeDtypeStruct((rows, width), F32),
             jax.ShapeDtypeStruct((experts // 2, 2, rows, 2 * cap), BF16),
         ),
-        in_specs=[VMEM] * 7,
+        in_specs=[SMEM] + [VMEM] * 6,
         out_specs=(VMEM, VMEM, VMEM),
-        compiler_params=pltpu.CompilerParams(vmem_limit_bytes=VMEM_LIMIT),
-    )(q, own, sib, residual, router_t, ids, ids.T)
+        scratch_shapes=[
+            pltpu.VMEM((n_branch - 1, rows, own.shape[2]), BF16),
+            pltpu.VMEM((n_branch - 1, rows, own.shape[2]), BF16),
+            pltpu.VMEM((halves, 2 * rows, 1), F32),
+            pltpu.VMEM((halves, 2 * rows, 1), F32),
+            pltpu.SemaphoreType.DMA((n_branch,)),
+            pltpu.SemaphoreType.DMA((n_branch,)),
+        ],
+        compiler_params=pltpu.CompilerParams(
+            collective_id=0, has_side_effects=True, vmem_limit_bytes=VMEM_LIMIT
+        ),
+    )(listed, q, own, residual, router_t, ids, ids.T)
 
 
 def expert_kernel(
@@ -369,12 +368,15 @@
     capacity = 2 * ((3 * rows * top_count + 4 * experts - 1) // (4 * experts))
     cap = (capacity + 15) // 16 * 16
     kv = keyvals.reshape(rows, -1)
-    own, sib = exchange_kv(kv, read_list.reshape(-1), n_branch, n_seq)
-    own = own.reshape(-1, kv.shape[1])
-    sib = sib.reshape(-1, kv.shape[1])
+    shifts = [
+        lax.ppermute(kv, "seq", [(i, (i + step) % n_seq) for i in range(n_seq)])
+        for step in range(1, n_seq)
+    ]
+    own = jnp.stack([kv] + shifts)
     wgu = jnp.swapaxes(w_gate_up[0], 0, 1)
     send, state, gate = attend(
-        queries[0], own, sib, residual[0], router.T, expert_ids[0], experts, cap, n_seq
+        read_list.reshape(-1), queries[0], own, residual[0], router.T, expert_ids[0],
+        experts, cap, n_branch, n_seq,
     )
     return run_experts(send, state, gate, wgu, w_down[0], experts, cap, n_seq)[None]
 

time: 198 us -> 192 us (0.970)
  Pallas kernels: 186 us -> 176 us
  starting transfers between devices: 0 us -> 3.25 us
    pallas_call x2 -> x1, Pallas kernels: 38.9 us -> 28.1 us  [attend(): pl.pallas_call(functools.partial(attend_kernel, experts, cap, n_branch, n...]
    ppermute x0 -> x3, starting transfers between devices: none -> 3.25 us  [on_device(): lax.ppermute(kv, 'seq', [(i, (i + step) % n_seq) for i in range(n_seq)])]
  transfers between devices with their start and end apart: 0 -> 3, of which waited for: 0 -> 0; matrix products, arithmetic and copies ran while one was open for 0% -> 5% of each run, Pallas kernels for 0% -> 0%
where the time goes in v2:
time: 192 us
  Pallas kernels  176 us (92%)
  local copies, waits for them, and re-layouts  11.8 us (6%)
  starting transfers between devices  3.25 us (2%)
    pallas_call x1, Pallas kernels, run_experts(): pl.pallas_call(functools.partial(expert_kernel, experts, cap, n_seq), out...  147 us
    pallas_call x1, Pallas kernels, attend(): pl.pallas_call(functools.partial(attend_kernel, experts, cap, n_branch, n...  28.1 us
    unnamed x3, local copies, waits for them, and re-layouts  9.44 us
  transfers between devices with their start and end apart: 3, of which 0 were waited for; matrix products, arithmetic and copies ran while one was open for 5% of the time, Pallas kernels for 0%

profile of v2, /device:TPU:0, one launch (start us, length us, event | category | flops | bytes accessed | tf_op | source)
XLA Modules:
  0.0 191.6 jit_solution(10747069907312918104)
XLA Ops:
  0.0 0.9 copy.11
  0.9 2.5 %collective-permute-start.2 = (bf16[128,512]{1,0:T(8,128)(2,1)S(1)}, bf16[128,512]{1,0:T(8,128)(2,1)S(1)}, u32[]{:S(2)}, u32[]{:S(2)}) collective-permute-start(bf16[128,512]{1,0:T(8,128)(2,1)S(1)} %bitcast.26), channel_id=1, source_target_pairs={{0,3},{1,0},{2,1},{3,2},{4,7},{5,4},{6,5},{7,6},{8,11},{9,8},{10,9... | collective-permute-start | bytes 393224 | tf_op jit(solution)/shard_map/ppermute | solution.py:372
  3.4 0.6 collective-permute-start.1
  4.0 0.2 collective-permute-start
  4.2 1.0 stack_reshape.3
  5.2 1.4 copy.9.ids_ref
  6.6 6.2 %copy.13 = bf16[1,4096,2,384]{3,1,2,0:T(8,128)(2,1)} copy(bf16[1,4096,2,384]{3,2,1,0:T(2,128)(2,1)} %param.14) | data formatting | bytes 12582912 | tf_op args[6]
  12.8 0.0 collective-permute-done.2
  12.8 0.0 collective-permute-done.1
  12.8 0.0 collective-permute-done
  12.8 0.9 pad_maximum_fusion.own_ref
  13.7 28.1 %shard_map.82 = (bf16[384,4096]{1,0:T(8,128)(2,1)}, f32[128,4096]{1,0:T(8,128)}, bf16[4,2,128,96]{3,2,1,0:T(8,128)(2,1)}) custom-call(s32[3]{0:T(128)} %bitcast.35, bf16[128,4096]{1,0:T(8,128)(2,1)} %bitcast.23, bf16[4,128,512]{2,1,0:T(8,128)(2,1)} %pad_maximum_fusion.own_ref, bf16[128,4096]{1,0:T(8,128)(2,1)} %bitcast.24, bf16[8,4096]{1,0:T(8,128)(2,1)} %bitcast.32, ...), custom_call_target="tpu_custom_call" | custom-call | tf_op jit(solution)/shard_map/pallas_call | solution.py:175
  41.8 147.4 %shard_map.83 = bf16[128,4096]{1,0:T(8,128)(2,1)} custom-call(bf16[384,4096]{1,0:T(8,128)(2,1)} %get-tuple-element.8.send_ref, f32[128,4096]{1,0:T(8,128)} %get-tuple-element.9.state_ref, bf16[4,2,128,96]{3,2,1,0:T(8,128)(2,1)} %get-tuple-element.10.gate_ref, bf16[2,4096,384]{2,1,0:T(8,128)(2,1)} %bitcast.20, bf16[384,4096]{1,0:T(8,128)(2,1)} %bitcast.22), custom_call_target="tpu_custom_call" | custom-call | tf_op jit(solution)/shard_map/pallas_call | solution.py:335
  189.3 2.3 %copy.15 = bf16[1,128,4096]{2,1,0:T(8,128)(2,1)} copy(bf16[1,128,4096]{2,1,0:T(8,128)(2,1)} %bitcast.21) | data formatting | bytes 2097152
Async XLA Ops:
  0.9 11.9 %collective-permute-start.2 = (bf16[128,512]{1,0:T(8,128)(2,1)S(1)}, bf16[128,512]{1,0:T(8,128)(2,1)S(1)}, u32[]{:S(2)}, u32[]{:S(2)}) collective-permute-start(bf16[128,512]{1,0:T(8,128)(2,1)S(1)} %bitcast.26), channel_id=1, source_target_pairs={{0,3},{1,0},{2,1},{3,2},{4,7},{5,4},{6,5},{7,6},{8,11},{9,8},{10,9... | collective-permute-start | bytes 393224 | tf_op jit(solution)/shard_map/ppermute | solution.py:372
  3.4 9.4 %collective-permute-start.1 = (bf16[128,512]{1,0:T(8,128)(2,1)S(1)}, bf16[128,512]{1,0:T(8,128)(2,1)S(1)}, u32[]{:S(2)}, u32[]{:S(2)}) collective-permute-start(bf16[128,512]{1,0:T(8,128)(2,1)S(1)} %bitcast.27), channel_id=1, source_target_pairs={{0,2},{1,3},{2,0},{3,1},{4,6},{5,7},{6,4},{7,5},{8,10},{9,11},{10,... | collective-permute-start | bytes 393224 | tf_op jit(solution)/shard_map/ppermute | solution.py:372
  4.0 8.8 %collective-permute-start = (bf16[128,512]{1,0:T(8,128)(2,1)S(1)}, bf16[128,512]{1,0:T(8,128)(2,1)S(1)}, u32[]{:S(2)}, u32[]{:S(2)}) collective-permute-start(bf16[128,512]{1,0:T(8,128)(2,1)S(1)} %bitcast.28), channel_id=1, source_target_pairs={{0,1},{1,2},{2,3},{3,0},{4,5},{5,6},{6,7},{7,4},{8,9},{9,10},{10,1... | collective-permute-start | bytes 393224 | tf_op jit(solution)/shard_map/ppermute | solution.py:372

commit v3 on v2

--- a/solution.py
+++ b/solution.py
@@ -9,6 +9,7 @@
 from jax.sharding import PartitionSpec as P
 
 HEAD_SIZE = 128
+PARTS = 4
 VMEM_LIMIT = 60 * 1024 * 1024
 F32 = jnp.float32
 BF16 = jnp.bfloat16
@@ -28,7 +29,7 @@
 def attend_kernel(
     experts, cap, n_branch, n_seq,
     list_ref, q_ref, own_ref, res_ref, router_ref, ids_ref, idt_ref,
-    send_ref, state_ref, gate_ref,
+    send_ref, state_ref, gate_ref, norm_ref, meta_ref,
     picked, sib_ref, tops, totals, ssem, rsem,
 ):
     branch = lax.axis_index("branch")
@@ -153,10 +154,22 @@
     chosen = [jnp.sum(logits * hot[k], axis=1, keepdims=True) for k in range(top_count)]
     gates = [1.0 / sum(jnp.exp(c - chosen[k]) for c in chosen) for k in range(top_count)]
 
+    parts, _, part_width = norm_ref.shape
+    for c in range(parts):
+        norm_ref[c] = normed[:, c * part_width : (c + 1) * part_width]
+    logits_t = lax.dot_general(router_ref[...], normed, nt, preferred_element_type=F32)
+    chosen_t = [jnp.sum(logits_t * hot_t[k], axis=0, keepdims=True) for k in range(top_count)]
+    meta_ref[...] = jnp.zeros_like(meta_ref)
+    for k in range(top_count):
+        meta_ref[k : k + 1, :] = dest_t[k].astype(F32)
+        meta_ref[top_count + k : top_count + k + 1, :] = 1.0 / sum(
+            jnp.exp(c - chosen_t[k]) for c in chosen_t
+        )
+
     pair = 2 * cap
     places = lax.broadcasted_iota(jnp.int32, (rows, pair), 1)
     places_t = lax.broadcasted_iota(jnp.int32, (pair, rows), 0)
-    for p in range(experts // 2):
+    for p in range(send_ref.shape[0] // pair):
         pick = sum((dest_t[k] - p * pair == places_t).astype(F32) for k in range(top_count))
         send_ref[p * pair : (p + 1) * pair, :] = jnp.dot(
             pick.astype(BF16), normed, preferred_element_type=F32
@@ -169,18 +182,20 @@
         gate_ref[p, 1] = (weight - high.astype(F32)).astype(BF16)
 
 
-def attend(listed, q, own, residual, router_t, ids, experts, cap, n_branch, n_seq):
+def attend(listed, q, own, residual, router_t, ids, experts, near, cap, n_branch, n_seq):
     rows, width = q.shape
     halves = width // HEAD_SIZE // 2
     return pl.pallas_call(
         functools.partial(attend_kernel, experts, cap, n_branch, n_seq),
         out_shape=(
-            jax.ShapeDtypeStruct((experts * cap, width), BF16),
+            jax.ShapeDtypeStruct((near * cap, width), BF16),
             jax.ShapeDtypeStruct((rows, width), F32),
-            jax.ShapeDtypeStruct((experts // 2, 2, rows, 2 * cap), BF16),
+            jax.ShapeDtypeStruct((near // 2, 2, rows, 2 * cap), BF16),
+            jax.ShapeDtypeStruct((PARTS, rows, width // PARTS), BF16),
+            jax.ShapeDtypeStruct((8, rows), F32),
         ),
         in_specs=[SMEM] + [VMEM] * 6,
-        out_specs=(VMEM, VMEM, VMEM),
+        out_specs=(VMEM,) * 5,
         scratch_shapes=[
             pltpu.VMEM((n_branch - 1, rows, own.shape[2]), BF16),
             pltpu.VMEM((n_branch - 1, rows, own.shape[2]), BF16),
@@ -359,6 +374,282 @@
     )(send, state, gate, wgu, wdn)
 
 
+def relay_kernel(
+    cap, n_seq,
+    send_ref, state_ref, gate_ref, norm_ref, meta_ref, wgu_ref, wdn_ref, out_ref,
+    recv, res, ret, wgu, wdn, acc, xin, xmeta, fwd, rbuf, xout, far,
+    wsend, wrecv, wloc, lsem, dsend, drecv, bsend, brecv,
+    csend, crecv, msend, mrecv, fsend, rsend, rrecv, osend, orecv,
+):
+    experts, near = 8, 4
+    branch = lax.axis_index("branch")
+    seq = lax.axis_index("seq")
+    core = seq % 2
+    me = (branch * n_seq + seq) // 2
+    inner = (branch + 1) // 2 % 2
+    pair = 2 * cap
+    rows, width = state_ref.shape
+    step = width // PARTS
+    twin = {"seq": seq + 1 - 2 * core}
+    mesh_id = pl.DeviceIdType.MESH
+
+    def place(k):
+        other = flipped(me, k, experts)
+        return {"branch": (2 * other) // n_seq, "seq": (2 * other) % n_seq + core}
+
+    barrier = pltpu.get_barrier_semaphore()
+    pl.semaphore_signal(barrier, inc=1, device_id=twin, device_id_type=mesh_id)
+    for k in range(1, experts):
+        pl.semaphore_signal(barrier, inc=1, device_id=place(k), device_id_type=mesh_id)
+    pl.semaphore_wait(barrier, experts)
+
+    def block(k):
+        return pl.ds(pl.multiple_of(k * cap, 16), cap)
+
+    def remote(src, dst, send, arrive, k):
+        return pltpu.make_async_remote_copy(
+            src_ref=src, dst_ref=dst, send_sem=send, recv_sem=arrive,
+            device_id=place(k), device_id_type=mesh_id,
+        )
+
+    def dispatch(k):
+        return remote(send_ref.at[block(k)], recv.at[block(k)], dsend.at[k], drecv.at[k], k)
+
+    def give_back(k):
+        return remote(res.at[block(k)], ret.at[block(k)], bsend.at[k], brecv.at[k], k)
+
+    across = 4 + 2 * inner
+
+    def cross(c):
+        return remote(norm_ref.at[c], xin.at[1 - inner, c], csend.at[c], crecv.at[1 - inner, c], across)
+
+    def cross_meta():
+        return remote(meta_ref, xmeta.at[1 - inner], msend, mrecv.at[1 - inner], across)
+
+    def arrived(s, c):
+        return remote(norm_ref.at[c], xin.at[s, c], csend.at[c], crecv.at[s, c], across)
+
+    def slot_of(s, f):
+        return f ^ (6 - 2 * s)
+
+    def part(c):
+        return slice(c * step, (c + 1) * step)
+
+    def forward(s, f, c):
+        k = slot_of(s, f)
+        src = fwd.at[s, f, :, part(c)]
+        dst = recv.at[block(k), part(c)]
+        if f == 0:
+            return pltpu.make_async_copy(src, dst, drecv.at[k])
+        return remote(src, dst, fsend.at[s, f], drecv.at[k], f)
+
+    def got(k):
+        remote(recv.at[block(k)], recv.at[block(k)], dsend.at[k], drecv.at[k], 1).wait_recv()
+
+    weights = []
+    for i, (src, dst) in enumerate(((wgu_ref, wgu), (wdn_ref, wdn))):
+        weights.append(
+            pltpu.make_async_remote_copy(
+                src_ref=src, dst_ref=dst.at[1], send_sem=wsend.at[i], recv_sem=wrecv.at[i],
+                device_id=twin, device_id_type=mesh_id,
+            )
+        )
+        weights.append(pltpu.make_async_copy(src, dst.at[0], wloc.at[i]))
+
+    def start_cross():
+        cross_meta().start()
+        for c in range(PARTS):
+            cross(c).start()
+
+    pl.when(inner == 1)(start_cross)
+    mine = pltpu.make_async_copy(send_ref.at[block(0)], recv.at[block(0)], lsem)
+    mine.start()
+    for k in (1, 2, 3):
+        dispatch(k).start()
+    pl.when(inner == 0)(start_cross)
+    for copy in weights:
+        copy.start()
+    acc[...] = state_ref[...]
+
+    def rows_of(s):
+        where = lax.broadcasted_iota(jnp.int32, (cap, rows), 0).astype(F32)
+        meta = xmeta[s]
+        return meta, [where + float(slot_of(s, f) * cap) for f in range(near)]
+
+    def relay(s):
+        remote(meta_ref, xmeta.at[s], msend, mrecv.at[s], across).wait_recv()
+        meta, where = rows_of(s)
+        pick = jnp.concatenate(
+            [(meta[0:1] == w).astype(F32) + (meta[1:2] == w).astype(F32) for w in where], axis=0
+        ).astype(BF16)
+        for c in range(PARTS):
+            arrived(s, c).wait_recv()
+            taken = jnp.dot(pick, xin[s, c], preferred_element_type=F32).astype(BF16)
+            for f in range(near):
+                fwd[s, f, :, part(c)] = taken[f * cap : (f + 1) * cap]
+            for f in (2, 3, 1, 0):
+                forward(s, f, c).start()
+
+    def hand(s, f, c, k):
+        src = res.at[block(k), part(c)]
+        dst = rbuf.at[s, f, :, part(c)]
+        if f == 0:
+            return pltpu.make_async_copy(src, dst, rrecv.at[s, f, c])
+        return remote(src, dst, rsend.at[s, f, c], rrecv.at[s, f, c], f)
+
+    def compute(p, after=None):
+        span = pl.ds(pl.multiple_of(p * pair, 16), pair)
+        acts = []
+        for h in range(2):
+            x = recv[span, :]
+            gate = jnp.dot(x, wgu[h, 0], preferred_element_type=F32)
+            up = jnp.dot(x, wgu[h, 1], preferred_element_type=F32)
+            acts.append((gate / (1.0 + jnp.exp(-gate)) * up).astype(BF16))
+        for c in range(PARTS):
+            done = jnp.dot(acts[0], wdn[0, :, part(c)], preferred_element_type=F32)
+            done += jnp.dot(acts[1], wdn[1, :, part(c)], preferred_element_type=F32)
+            res[span, part(c)] = done.astype(BF16)
+            if after is not None:
+                after(c)
+
+    pl.when(inner == 1)(lambda: relay(0))
+    for copy in weights:
+        copy.wait()
+    mine.wait()
+    got(1)
+    compute(0)
+    give_back(1).start()
+    got(2)
+    got(3)
+    compute(1)
+    give_back(2).start()
+    give_back(3).start()
+    pl.when(inner == 1)(lambda: relay(1))
+
+    def far_group(s, base):
+        def after(c):
+            for f in (base, base + 1):
+                hand(s, f, c, slot_of(s, f)).start()
+
+        k = slot_of(s, base) // 2 * 2
+        got(k)
+        got(k + 1)
+        compute(k // 2, after)
+
+    for s in range(2):
+        pl.when(inner == 1)(functools.partial(far_group, s, 0))
+        pl.when(inner == 0)(functools.partial(far_group, s, 2))
+
+    def result(s, c):
+        return remote(xout.at[s, c], far.at[c], osend.at[s, c], orecv.at[c], 6 - 2 * s)
+
+    def combine(s):
+        meta, where = rows_of(s)
+        weight = jnp.concatenate(
+            [
+                jnp.where(meta[0:1] == w, meta[2:3], 0.0) + jnp.where(meta[1:2] == w, meta[3:4], 0.0)
+                for w in where
+            ],
+            axis=0,
+        ).T
+        high = weight.astype(BF16)
+        low = (weight - high.astype(F32)).astype(BF16)
+        for c in range(PARTS):
+            for f in range(near):
+                if f == 0:
+                    hand(s, 0, c, slot_of(s, 0)).wait()
+                else:
+                    hand(s, f, c, slot_of(s, f)).wait_recv()
+            given = rbuf[s, :, :, part(c)].reshape(near * cap, step)
+            xout[s, c] = (
+                jnp.dot(high, given, preferred_element_type=F32)
+                + jnp.dot(low, given, preferred_element_type=F32)
+            ).astype(BF16)
+            result(s, c).start()
+
+    def combine_all():
+        combine(0)
+        combine(1)
+
+    pl.when(inner == 1)(combine_all)
+
+    for p in range(near // 2):
+        for k in (2 * p, 2 * p + 1):
+            if k:
+                give_back(k).wait_recv()
+        for c in range(PARTS):
+            cols = part(c)
+            low = res if p == 0 else ret
+            given = jnp.concatenate(
+                [low[2 * p * cap : (2 * p + 1) * cap, cols], ret[(2 * p + 1) * cap : (2 * p + 2) * cap, cols]],
+                axis=0,
+            )
+            acc[:, cols] += jnp.dot(gate_ref[p, 0], given, preferred_element_type=F32) + jnp.dot(
+                gate_ref[p, 1], given, preferred_element_type=F32
+            )
+    for c in range(PARTS):
+        result(0, c).wait_recv()
+        out_ref[:, part(c)] = (acc[:, part(c)] + far[c].astype(F32)).astype(BF16)
+
+    for k in (1, 2, 3):
+        dispatch(k).wait_send()
+        give_back(k).wait_send()
+    cross_meta().wait_send()
+    for c in range(PARTS):
+        cross(c).wait_send()
+
+    def inner_end():
+        for s in range(2):
+            for f in (1, 2, 3):
+                remote(fwd.at[s, f], fwd.at[s, f], fsend.at[s, f], drecv.at[0], f).wait_send()
+            for c in range(PARTS):
+                hand(s, 1, c, slot_of(s, 1)).wait_send()
+                result(s, c).wait_send()
+
+    def outer_end():
+        for s in range(2):
+            for f in (2, 3):
+                for c in range(PARTS):
+                    hand(s, f, c, slot_of(s, f)).wait_send()
+
+    pl.when(inner == 1)(inner_end)
+    pl.when(inner == 0)(outer_end)
+
+
+def run_relayed(send, state, gate, normed, meta, wgu, wdn, cap, n_seq):
+    rows, width = state.shape
+    ff = wdn.shape[0]
+    part = width // PARTS
+    dma = pltpu.SemaphoreType.DMA
+    return pl.pallas_call(
+        functools.partial(relay_kernel, cap, n_seq),
+        out_shape=jax.ShapeDtypeStruct((rows, width), BF16),
+        in_specs=[ANY, VMEM, VMEM, ANY, VMEM, ANY, ANY],
+        out_specs=VMEM,
+        scratch_shapes=[
+            pltpu.VMEM((8 * cap, width), BF16),
+            pltpu.VMEM((8 * cap, width), BF16),
+            pltpu.VMEM((4 * cap, width), BF16),
+            pltpu.VMEM((2, 2, width, ff), BF16),
+            pltpu.VMEM((2, ff, width), BF16),
+            pltpu.VMEM((rows, width), F32),
+            pltpu.VMEM((2, PARTS, rows, part), BF16),
+            pltpu.VMEM((2, 8, rows), F32),
+            pltpu.VMEM((2, 4, cap, width), BF16),
+            pltpu.VMEM((2, 4, cap, width), BF16),
+            pltpu.VMEM((2, PARTS, rows, part), BF16),
+            pltpu.VMEM((PARTS, rows, part), BF16),
+            dma((2,)), dma((2,)), dma((2,)), dma,
+            dma((8,)), dma((8,)), dma((8,)), dma((8,)),
+            dma((PARTS,)), dma((2, PARTS)), dma, dma((2,)), dma((2, 4)),
+            dma((2, 4, PARTS)), dma((2, 4, PARTS)), dma((2, PARTS)), dma((PARTS,)),
+        ],
+        compiler_params=pltpu.CompilerParams(
+            collective_id=2, has_side_effects=True, vmem_limit_bytes=VMEM_LIMIT
+        ),
+    )(send, state, gate, normed, meta, wgu, wdn)
+
+
 def on_device(
     n_branch, n_seq, queries, keyvals, residual, read_list, router, expert_ids, w_gate_up, w_down
 ):
@@ -374,10 +665,14 @@
     ]
     own = jnp.stack([kv] + shifts)
     wgu = jnp.swapaxes(w_gate_up[0], 0, 1)
-    send, state, gate = attend(
+    line = n_branch == 4 and n_seq == 4 and experts == 8 and top_count == 2
+    near = 4 if line else experts
+    send, state, gate, normed, meta = attend(
         read_list.reshape(-1), queries[0], own, residual[0], router.T, expert_ids[0],
-        experts, cap, n_branch, n_seq,
+        experts, near, cap, n_branch, n_seq,
     )
+    if line:
+        return run_relayed(send, state, gate, normed, meta, wgu, w_down[0], cap, n_seq)[None]
     return run_experts(send, state, gate, wgu, w_down[0], experts, cap, n_seq)[None]
 
 

time: 192 us -> 188 us (0.979)
  Pallas kernels: 176 us -> 172 us
    pallas_call x1, Pallas kernels: 147 us -> 144 us  [run_relayed(): pl.pallas_call(functools.partial(relay_kernel, cap, n_seq), out_shape=jax...]
where the time goes in v3:
time: 188 us
  Pallas kernels  172 us (91%)
  local copies, waits for them, and re-layouts  11.8 us (6%)
  starting transfers between devices  3.25 us (2%)
    pallas_call x1, Pallas kernels, run_relayed(): pl.pallas_call(functools.partial(relay_kernel, cap, n_seq), out_shape=jax...  144 us
    pallas_call x1, Pallas kernels, attend(): pl.pallas_call(functools.partial(attend_kernel, experts, cap, n_branch, n...  27.5 us
    unnamed x3, local copies, waits for them, and re-layouts  9.44 us
  transfers between devices with their start and end apart: 3, of which 0 were waited for; matrix products, arithmetic and copies ran while one was open for 5% of the time, Pallas kernels for 0%

profile of v3, /device:TPU:0, one launch (start us, length us, event | category | flops | bytes accessed | tf_op | source)
XLA Modules:
  0.0 188.0 jit_solution(17547731840055901950)
XLA Ops:
  0.0 0.9 copy.11
  0.9 2.5 %collective-permute-start.2 = (bf16[128,512]{1,0:T(8,128)(2,1)S(1)}, bf16[128,512]{1,0:T(8,128)(2,1)S(1)}, u32[]{:S(2)}, u32[]{:S(2)}) collective-permute-start(bf16[128,512]{1,0:T(8,128)(2,1)S(1)} %bitcast.26), channel_id=1, source_target_pairs={{0,3},{1,0},{2,1},{3,2},{4,7},{5,4},{6,5},{7,6},{8,11},{9,8},{10,9... | collective-permute-start | bytes 393224 | tf_op jit(solution)/shard_map/ppermute | solution.py:663
  3.4 0.6 collective-permute-start.1
  4.0 0.2 collective-permute-start
  4.2 1.0 stack_reshape.3
  5.2 1.4 copy.9.ids_ref
  6.6 6.2 %copy.13 = bf16[1,4096,2,384]{3,1,2,0:T(8,128)(2,1)} copy(bf16[1,4096,2,384]{3,2,1,0:T(2,128)(2,1)} %param.14) | data formatting | bytes 12582912 | tf_op args[6]
  12.8 0.0 collective-permute-done.2
  12.8 0.0 collective-permute-done.1
  12.8 0.0 collective-permute-done
  12.8 0.9 pad_maximum_fusion.own_ref
  13.7 27.5 %shard_map.82 = (bf16[192,4096]{1,0:T(8,128)(2,1)}, f32[128,4096]{1,0:T(8,128)}, bf16[2,2,128,96]{3,2,1,0:T(8,128)(2,1)}, bf16[4,128,1024]{2,1,0:T(8,128)(2,1)}, f32[8,128]{1,0:T(8,128)}) custom-call(s32[3]{0:T(128)} %bitcast.35, bf16[128,4096]{1,0:T(8,128)(2,1)} %bitcast.23, bf16[4,128,512]{2,1,0:T(8,128)(2,1)} %pad_maximum_fusion.own_ref, ...), custom_call_target="tpu_custom_call" | custom-call | tf_op jit(solution)/shard_map/pallas_call | solution.py:188
  41.2 144.5 %shard_map.83 = bf16[128,4096]{1,0:T(8,128)(2,1)} custom-call(bf16[192,4096]{1,0:T(8,128)(2,1)} %get-tuple-element.10.send_ref, f32[128,4096]{1,0:T(8,128)} %get-tuple-element.11.state_ref, bf16[2,2,128,96]{3,2,1,0:T(8,128)(2,1)} %get-tuple-element.12.gate_ref, bf16[4,128,1024]{2,1,0:T(8,128)(2,1)} %get-tuple-element.13.norm_ref, ...), custom_call_target="tpu_custom_call" | custom-call | tf_op jit(solution)/shard_map/pallas_call | solution.py:624
  185.7 2.3 %copy.15 = bf16[1,128,4096]{2,1,0:T(8,128)(2,1)} copy(bf16[1,128,4096]{2,1,0:T(8,128)(2,1)} %bitcast.21) | data formatting | bytes 2097152
Async XLA Ops:
  0.9 11.9 %collective-permute-start.2 = (bf16[128,512]{1,0:T(8,128)(2,1)S(1)}, bf16[128,512]{1,0:T(8,128)(2,1)S(1)}, u32[]{:S(2)}, u32[]{:S(2)}) collective-permute-start(bf16[128,512]{1,0:T(8,128)(2,1)S(1)} %bitcast.26), channel_id=1, source_target_pairs={{0,3},{1,0},{2,1},{3,2},{4,7},{5,4},{6,5},{7,6},{8,11},{9,8},{10,9... | collective-permute-start | bytes 393224 | tf_op jit(solution)/shard_map/ppermute | solution.py:663
  3.4 9.4 %collective-permute-start.1 = (bf16[128,512]{1,0:T(8,128)(2,1)S(1)}, bf16[128,512]{1,0:T(8,128)(2,1)S(1)}, u32[]{:S(2)}, u32[]{:S(2)}) collective-permute-start(bf16[128,512]{1,0:T(8,128)(2,1)S(1)} %bitcast.27), channel_id=1, source_target_pairs={{0,2},{1,3},{2,0},{3,1},{4,6},{5,7},{6,4},{7,5},{8,10},{9,11},{10,... | collective-permute-start | bytes 393224 | tf_op jit(solution)/shard_map/ppermute | solution.py:663
  4.0 8.8 %collective-permute-start = (bf16[128,512]{1,0:T(8,128)(2,1)S(1)}, bf16[128,512]{1,0:T(8,128)(2,1)S(1)}, u32[]{:S(2)}, u32[]{:S(2)}) collective-permute-start(bf16[128,512]{1,0:T(8,128)(2,1)S(1)} %bitcast.28), channel_id=1, source_target_pairs={{0,1},{1,2},{2,3},{3,0},{4,5},{5,6},{6,7},{7,4},{8,9},{9,10},{10,1... | collective-permute-start | bytes 393224 | tf_op jit(solution)/shard_map/ppermute | solution.py:663

commit v4 on v3

--- a/solution.py
+++ b/solution.py
@@ -461,14 +461,14 @@
         for c in range(PARTS):
             cross(c).start()
 
+    for copy in weights:
+        copy.start()
     pl.when(inner == 1)(start_cross)
     mine = pltpu.make_async_copy(send_ref.at[block(0)], recv.at[block(0)], lsem)
     mine.start()
     for k in (1, 2, 3):
         dispatch(k).start()
     pl.when(inner == 0)(start_cross)
-    for copy in weights:
-        copy.start()
     acc[...] = state_ref[...]
 
     def rows_of(s):
@@ -519,11 +519,6 @@
     got(1)
     compute(0)
     give_back(1).start()
-    got(2)
-    got(3)
-    compute(1)
-    give_back(2).start()
-    give_back(3).start()
     pl.when(inner == 1)(lambda: relay(1))
 
     def far_group(s, base):
@@ -567,11 +562,13 @@
             ).astype(BF16)
             result(s, c).start()
 
-    def combine_all():
-        combine(0)
-        combine(1)
-
-    pl.when(inner == 1)(combine_all)
+    pl.when(inner == 1)(lambda: combine(0))
+    got(2)
+    got(3)
+    compute(1)
+    give_back(2).start()
+    give_back(3).start()
+    pl.when(inner == 1)(lambda: combine(1))
 
     for p in range(near // 2):
         for k in (2 * p, 2 * p + 1):

time: 188 us -> 191 us (1.016)
  Pallas kernels: 172 us -> 175 us
    pallas_call x1, Pallas kernels: 144 us -> 147 us  [run_relayed(): pl.pallas_call(functools.partial(relay_kernel, cap, n_seq), out_shape=jax...]
where the time goes in v4:
time: 191 us
  Pallas kernels  175 us (92%)
  local copies, waits for them, and re-layouts  11.8 us (6%)
  starting transfers between devices  3.25 us (2%)
    pallas_call x1, Pallas kernels, run_relayed(): pl.pallas_call(functools.partial(relay_kernel, cap, n_seq), out_shape=jax...  147 us
    pallas_call x1, Pallas kernels, attend(): pl.pallas_call(functools.partial(attend_kernel, experts, cap, n_branch, n...  27.5 us
    unnamed x3, local copies, waits for them, and re-layouts  9.44 us
  transfers between devices with their start and end apart: 3, of which 0 were waited for; matrix products, arithmetic and copies ran while one was open for 5% of the time, Pallas kernels for 0%

profile of v4, /device:TPU:0, one launch (start us, length us, event | category | flops | bytes accessed | tf_op | source)
XLA Modules:
  0.0 190.7 jit_solution(8633352278764898875)
XLA Ops:
  0.0 0.9 copy.11
  0.9 2.5 %collective-permute-start.2 = (bf16[128,512]{1,0:T(8,128)(2,1)S(1)}, bf16[128,512]{1,0:T(8,128)(2,1)S(1)}, u32[]{:S(2)}, u32[]{:S(2)}) collective-permute-start(bf16[128,512]{1,0:T(8,128)(2,1)S(1)} %bitcast.26), channel_id=1, source_target_pairs={{0,3},{1,0},{2,1},{3,2},{4,7},{5,4},{6,5},{7,6},{8,11},{9,8},{10,9... | collective-permute-start | bytes 393224 | tf_op jit(solution)/shard_map/ppermute | solution.py:660
  3.4 0.6 collective-permute-start.1
  4.0 0.2 collective-permute-start
  4.2 1.0 stack_reshape.3
  5.2 1.4 copy.9.ids_ref
  6.6 6.2 %copy.13 = bf16[1,4096,2,384]{3,1,2,0:T(8,128)(2,1)} copy(bf16[1,4096,2,384]{3,2,1,0:T(2,128)(2,1)} %param.14) | data formatting | bytes 12582912 | tf_op args[6]
  12.8 0.0 collective-permute-done.2
  12.8 0.0 collective-permute-done.1
  12.8 0.0 collective-permute-done
  12.8 0.9 pad_maximum_fusion.own_ref
  13.7 27.5 %shard_map.82 = (bf16[192,4096]{1,0:T(8,128)(2,1)}, f32[128,4096]{1,0:T(8,128)}, bf16[2,2,128,96]{3,2,1,0:T(8,128)(2,1)}, bf16[4,128,1024]{2,1,0:T(8,128)(2,1)}, f32[8,128]{1,0:T(8,128)}) custom-call(s32[3]{0:T(128)} %bitcast.35, bf16[128,4096]{1,0:T(8,128)(2,1)} %bitcast.23, bf16[4,128,512]{2,1,0:T(8,128)(2,1)} %pad_maximum_fusion.own_ref, ...), custom_call_target="tpu_custom_call" | custom-call | tf_op jit(solution)/shard_map/pallas_call | solution.py:188
  41.2 147.1 %shard_map.83 = bf16[128,4096]{1,0:T(8,128)(2,1)} custom-call(bf16[192,4096]{1,0:T(8,128)(2,1)} %get-tuple-element.10.send_ref, f32[128,4096]{1,0:T(8,128)} %get-tuple-element.11.state_ref, bf16[2,2,128,96]{3,2,1,0:T(8,128)(2,1)} %get-tuple-element.12.gate_ref, bf16[4,128,1024]{2,1,0:T(8,128)(2,1)} %get-tuple-element.13.norm_ref, ...), custom_call_target="tpu_custom_call" | custom-call | tf_op jit(solution)/shard_map/pallas_call | solution.py:621
  188.4 2.3 %copy.15 = bf16[1,128,4096]{2,1,0:T(8,128)(2,1)} copy(bf16[1,128,4096]{2,1,0:T(8,128)(2,1)} %bitcast.21) | data formatting | bytes 2097152
Async XLA Ops:
  0.9 11.9 %collective-permute-start.2 = (bf16[128,512]{1,0:T(8,128)(2,1)S(1)}, bf16[128,512]{1,0:T(8,128)(2,1)S(1)}, u32[]{:S(2)}, u32[]{:S(2)}) collective-permute-start(bf16[128,512]{1,0:T(8,128)(2,1)S(1)} %bitcast.26), channel_id=1, source_target_pairs={{0,3},{1,0},{2,1},{3,2},{4,7},{5,4},{6,5},{7,6},{8,11},{9,8},{10,9... | collective-permute-start | bytes 393224 | tf_op jit(solution)/shard_map/ppermute | solution.py:660
  3.4 9.4 %collective-permute-start.1 = (bf16[128,512]{1,0:T(8,128)(2,1)S(1)}, bf16[128,512]{1,0:T(8,128)(2,1)S(1)}, u32[]{:S(2)}, u32[]{:S(2)}) collective-permute-start(bf16[128,512]{1,0:T(8,128)(2,1)S(1)} %bitcast.27), channel_id=1, source_target_pairs={{0,2},{1,3},{2,0},{3,1},{4,6},{5,7},{6,4},{7,5},{8,10},{9,11},{10,... | collective-permute-start | bytes 393224 | tf_op jit(solution)/shard_map/ppermute | solution.py:660
  4.0 8.8 %collective-permute-start = (bf16[128,512]{1,0:T(8,128)(2,1)S(1)}, bf16[128,512]{1,0:T(8,128)(2,1)S(1)}, u32[]{:S(2)}, u32[]{:S(2)}) collective-permute-start(bf16[128,512]{1,0:T(8,128)(2,1)S(1)} %bitcast.28), channel_id=1, source_target_pairs={{0,1},{1,2},{2,3},{3,0},{4,5},{5,6},{6,7},{7,4},{8,9},{9,10},{10,1... | collective-permute-start | bytes 393224 | tf_op jit(solution)/shard_map/ppermute | solution.py:660
